TPU v7x, 32 devices: a whole 2x2x4 slice. The times are simulated.
32 devices in a mesh: layer: 4 (over z), row: 4 (over x, core), col: 2 (over y).
Axes of the slice: x: 2, y: 2, z: 4, core: 2. Of those that a mesh axis runs over, the one named last changes fastest.
Arguments:
- rhs_low: bfloat16 [4, 2, 2, 384, 512], P('layer', None, 'col'), may hold values from -6 to 6
- inv_low: bfloat16 [4, 2, 2, 384, 384], P('layer', None, 'col'), as said below
- blocks: bfloat16 [4, 4, 2, 2, 4, 384, 384], P('layer', 'row', 'col'), may hold values from -0.02734375 to 0.02734375
- targets: int32 [4, 4, 2, 2, 4], P('layer', 'row', 'col'), may hold values from 1 to 5, as said below
- rhs_anc: bfloat16 [16, 384, 512], P('row', None, ('layer', 'col')), may hold values from -6 to 6
- inv_anc: bfloat16 [16, 384, 384], P('row'), as said below
Outputs:
- solution_low: bfloat16 [4, 2, 2, 384, 512], P('layer', None, 'col', None, 'row')
- solution_anc: float32 [16, 384, 512], P('row', None, ('layer', 'col'))
Inputs may be any that keep to these rules, and one draw needn't show every extreme that they name: For each g, r, c, l the 4 values targets[g, r, c, l, :] are distinct. A value t < 2 is greater than l; a value t >= 2 names ancestor r * 4 + t - 2. `inv_low`: each block is lower triangular. `inv_anc`: each block is lower triangular.
All inputs are finite; a program needn't handle non-finite values.
Results may differ from a plain program's by a relative error of at most 0.011.
Values may be sent and summed in bfloat16 or wider, within the bound.
A program may use at most 64 MiB of HBM per device.

v0:
```python
import jax
import jax.numpy as jnp
from jax import lax
from jax.sharding import PartitionSpec as P


def broadcast(value, axis, source):
    kept = jnp.where(lax.axis_index(axis) == source, value, 0).astype(value.dtype)
    return lax.psum(kept, axis)


def solve_block(inverse, right_side, partial_value):
    residual = (right_side.astype(jnp.float32) - partial_value).astype(jnp.bfloat16)
    return jnp.dot(inverse, residual, preferred_element_type=jnp.float32).astype(jnp.bfloat16)


def on_device(rhs_low, inv_low, blocks, targets, rhs_anc, inv_anc):
    row_index = lax.axis_index("row")
    column_index = lax.axis_index("col")
    grid_rows = lax.axis_size("row")
    levels = rhs_low.shape[1]
    block_width = inv_low.shape[-1]
    load_cases = rhs_low.shape[-1]
    per_row = blocks.shape[4]
    share = load_cases // grid_rows
    collected = jnp.zeros((levels + inv_anc.shape[0], block_width, load_cases), jnp.float32)
    pieces = []
    for current in range(levels):
        owner = (current + column_index) % grid_rows
        right_side = rhs_low[0, current, 0]
        inverse = inv_low[0, current, 0]
        if current == 0:
            nothing = jnp.zeros((block_width, load_cases), jnp.float32)
            answer = solve_block(inverse, right_side, nothing)
        else:
            summed = lax.psum(collected[current].astype(jnp.bfloat16), "col").astype(jnp.float32)
            answer = broadcast(solve_block(inverse, right_side, summed), "row", owner)
        pieces.append(lax.dynamic_slice_in_dim(answer, row_index * share, share, 1))
        stacked = blocks[0, 0, 0, current].reshape(per_row * block_width, block_width)
        product = jnp.dot(stacked, answer, preferred_element_type=jnp.float32).reshape(
            per_row, block_width, load_cases
        )
        for member in range(per_row):
            target = targets[0, 0, 0, current, member]
            before = lax.dynamic_index_in_dim(collected, target, 0, keepdims=False)
            collected = lax.dynamic_update_index_in_dim(
                collected, before + product[member], target, 0
            )
    solution_low = jnp.stack(pieces, 0)[None, :, None]
    ancestor_part = collected[levels:]
    merged = lax.psum_scatter(
        ancestor_part.astype(jnp.bfloat16), "layer", scatter_dimension=2, tiled=True
    ).astype(jnp.float32)
    merged = lax.psum_scatter(
        merged.astype(jnp.bfloat16), "col", scatter_dimension=2, tiled=True
    ).astype(jnp.float32)
    residual = (rhs_anc.astype(jnp.float32) - merged).astype(jnp.bfloat16)
    solution_anc = jnp.einsum("awv,avk->awk", inv_anc, residual, preferred_element_type=jnp.float32)
    return (solution_low, solution_anc)


def solution(mesh):
    in_specs = (
        P("layer", None, "col", None, None),
        P("layer", None, "col", None, None),
        P("layer", "row", "col", None, None, None, None),
        P("layer", "row", "col", None, None),
        P("row", None, ("layer", "col")),
        P("row", None, None),
    )
    out_specs = (P("layer", None, "col", None, "row"), P("row", None, ("layer", "col")))
    return jax.shard_map(
        on_device, mesh=mesh, in_specs=in_specs, out_specs=out_specs, check_vma=False
    )
```

profile of v0, /device:TPU:6, one launch (start us, length us, event | category | flops | bytes accessed | tf_op | source)
XLA Modules:
  0.0 170.8 jit_solution(2642291066755729662)
XLA Ops:
  7.2 0.0 copy-start
  7.2 0.0 all-reduce.3.cloned.1.call-start
  7.2 1.6 fusion.28
  13.9 1.9 %fusion.27 = (bf16[1,1,1,1,4,384,384]{6,5,4,3,2,1,0:T(8,128)(2,1)S(1)}, bf16[1,1,1,1,4,384,384]{6,5,4,3,2,1,0:T(8,128)(2,1)S(1)}) fusion(bf16[1,1,1,2,4,384,384]{6,5,4,3,2,1,0:T(8,128)(2,1)} %param.8), kind=kLoop, calls=%fused_computation.46 | loop fusion | bytes 4718592 | tf_op jit(solution)/shard_map/slice | solution.py:39
  16.4 1.4 convolution_convert_fusion.1
  17.8 0.0 copy-start.2
  17.8 0.8 copy-done.2
  18.6 2.7 %convolution_bitcast_fusion.1 = f32[1536,512]{0,1:T(8,128)} fusion(bf16[384,512]{1,0:T(8,128)(2,1)S(1)} %convolution_convert_fusion.1, bf16[1536,384]{1,0:T(8,128)(2,1)S(1)} %bitcast.94), kind=kOutput, calls=%fused_computation.1 | convolution fusion | flops 603979776 | bytes 4718592 | tf_op jit(solution)/shard_map/dot_general | solution.py:40
  22.0 0.0 copy-start.1
  22.0 2.6 %broadcast_in_dim.21 = f32[6,384,512]{1,2,0:T(8,128)} broadcast(f32[]{:T(128)} %constant.66.clone.1), dimensions={} | broadcast | bytes 4718596 | tf_op jit(solution)/shard_map/broadcast_in_dim | solution.py:26
  24.6 0.8 copy-done.1
  25.4 1.0 fusion.16
  26.4 2.1 %fusion.15 = f32[6,384,512]{1,2,0:T(8,128)} fusion(f32[6,384,512]{1,2,0:T(8,128)} %fusion.16, s32[]{:T(128)S(6)} %select_n.60, f32[1536,512]{0,1:T(8,128)S(1)} %copy-done.1), kind=kLoop, calls=%fused_computation.29 | loop fusion | flops 196608 | bytes 2359300 | tf_op jit(solution)/shard_map/jit(dynamic_update_index_in_dim)/dynamic_update_slice | solution.py:46
  29.1 0.0 slice-start
  29.1 2.4 %fusion.13 = f32[6,384,512]{1,2,0:T(8,128)} fusion(f32[6,384,512]{1,2,0:T(8,128)} %fusion.15, s32[]{:T(128)S(6)} %select_n.61, f32[1536,512]{0,1:T(8,128)} %convolution_bitcast_fusion.1), kind=kLoop, calls=%fused_computation.26 | loop fusion | flops 196608 | bytes 2359300 | tf_op jit(solution)/shard_map/jit(dynamic_update_index_in_dim)/dynamic_update_slice | solution.py:46
  32.1 2.3 %fusion.11 = f32[6,384,512]{1,2,0:T(8,128)} fusion(f32[6,384,512]{1,2,0:T(8,128)} %fusion.13, s32[]{:T(128)S(6)} %select_n.62, f32[1536,512]{0,1:T(8,128)} %convolution_bitcast_fusion.1), kind=kLoop, calls=%fused_computation.23 | loop fusion | flops 196608 | bytes 2359300 | tf_op jit(solution)/shard_map/jit(dynamic_update_index_in_dim)/dynamic_update_slice | solution.py:46
  34.5 1.9 %fusion.19 = bf16[384,512]{0,1:T(8,128)(2,1)} fusion(f32[6,384,512]{1,2,0:T(8,128)} %fusion.11), kind=kLoop, calls=%fused_computation.34 | loop fusion | bytes 786432 | tf_op jit(solution)/shard_map/convert_element_type | solution.py:36
  36.4 0.0 all-reduce.3.cloned.1.call-update
  36.4 0.0 all-reduce.5.cloned.1.call-start
  36.5 0.0 slice-done
  36.5 0.2 copy.12
  36.7 25.9 %all-reduce.3.cloned.1.call-done = bf16[384,512]{0,1:T(8,128)(2,1)} async-done(((bf16[384,512]{0,1:T(8,128)(2,1)}), bf16[384,512]{0,1:T(8,128)(2,1)}) %all-reduce.3.cloned.1.call-update) | async-done | bytes 393232 | tf_op jit(solution)/shard_map/psum | solution.py:36
  62.6 2.2 %fusion.1 = bf16[384,512]{0,1:T(8,128)(2,1)} fusion(bf16[384,512]{0,1:T(8,128)(2,1)} %all-reduce.3.cloned.1.call-done, bf16[1,1,1,384,512]{3,4,2,1,0:T(8,128)(2,1)S(1)} %copy.12, pred[]{:T(512)S(6)} %eq.5, bf16[1,2,1,384,384]{4,3,2,1,0:T(8,128)(2,1)} %param.7), kind=kOutput, calls=%fused_computation.7 | convolution fusion | flops 152174592 | bytes 1474561 | tf_op jit(solution)/shard_map/dot_general | solution.py:14
  64.8 0.0 all-reduce.5.cloned.1.call-update
  64.9 0.0 reduce-scatter.3.cloned.1.call-start
  72.3 26.0 %all-reduce.5.cloned.1.call-done = bf16[384,512]{0,1:T(8,128)(2,1)} async-done(((bf16[384,512]{0,1:T(8,128)(2,1)}), bf16[384,512]{0,1:T(8,128)(2,1)}) %all-reduce.5.cloned.1.call-update) | async-done | bytes 393232 | tf_op jit(solution)/shard_map/psum | solution.py:9
  98.3 2.0 %convolution_bitcast_fusion = f32[1536,512]{0,1:T(8,128)S(1)} fusion(bf16[384,512]{0,1:T(8,128)(2,1)} %all-reduce.5.cloned.1.call-done, bf16[1536,384]{1,0:T(8,128)(2,1)S(1)} %bitcast.93), kind=kOutput, calls=%fused_computation | convolution fusion | flops 603979776 | bytes 4718592 | tf_op jit(solution)/shard_map/dot_general | solution.py:40
  100.3 2.2 %fusion.9 = f32[6,384,512]{1,2,0:T(8,128)} fusion(f32[6,384,512]{1,2,0:T(8,128)} %fusion.11, s32[]{:T(128)S(6)} %select_n.65, f32[1536,512]{0,1:T(8,128)S(1)} %convolution_bitcast_fusion), kind=kLoop, calls=%fused_computation.19 | loop fusion | flops 196608 | bytes 2359300 | tf_op jit(solution)/shard_map/jit(dynamic_update_index_in_dim)/dynamic_update_slice | solution.py:46
  102.5 2.1 %fusion.7 = f32[6,384,512]{1,2,0:T(8,128)} fusion(f32[6,384,512]{1,2,0:T(8,128)} %fusion.9, s32[]{:T(128)S(6)} %select_n.66, f32[1536,512]{0,1:T(8,128)S(1)} %convolution_bitcast_fusion), kind=kLoop, calls=%fused_computation.16 | loop fusion | flops 196608 | bytes 2359300 | tf_op jit(solution)/shard_map/jit(dynamic_update_index_in_dim)/dynamic_update_slice | solution.py:46
  104.6 2.2 %fusion.5 = f32[6,384,512]{1,2,0:T(8,128)} fusion(f32[6,384,512]{1,2,0:T(8,128)} %fusion.7, s32[]{:T(128)S(6)} %select_n.67, f32[1536,512]{0,1:T(8,128)S(1)} %convolution_bitcast_fusion), kind=kLoop, calls=%fused_computation.13 | loop fusion | flops 196608 | bytes 2359300 | tf_op jit(solution)/shard_map/jit(dynamic_update_index_in_dim)/dynamic_update_slice | solution.py:46
  106.8 2.2 %fusion.3 = f32[6,384,512]{1,2,0:T(8,128)} fusion(f32[6,384,512]{1,2,0:T(8,128)} %fusion.5, s32[]{:T(128)S(6)} %select_n.68, f32[1536,512]{0,1:T(8,128)S(1)} %convolution_bitcast_fusion), kind=kLoop, calls=%fused_computation.10 | loop fusion | flops 196608 | bytes 2359300 | tf_op jit(solution)/shard_map/jit(dynamic_update_index_in_dim)/dynamic_update_slice | solution.py:46
  108.9 0.0 copy-start.3
  108.9 3.3 %slice.170 = bf16[4,384,512]{1,2,0:T(8,128)(2,1)} slice(f32[6,384,512]{1,2,0:T(8,128)} %fusion.3), slice={[2:6], [0:384], [0:512]} | slice | bytes 3145728 | tf_op jit(solution)/shard_map/slice | solution.py:50
  112.2 0.0 reduce-scatter.3.cloned.1.call-update
  112.2 0.0 reduce-scatter.5.cloned.1.call-start
  112.3 36.5 %reduce-scatter.3.cloned.1.call-done = bf16[4,384,128]{1,2,0:T(8,128)(2,1)} async-done(((bf16[4,384,512]{1,2,0:T(8,128)(2,1)}), bf16[4,384,128]{1,2,0:T(8,128)(2,1)}) %reduce-scatter.3.cloned.1.call-update) | async-done | bytes 393232 | tf_op jit(solution)/shard_map/reduce_scatter | solution.py:51
  148.8 0.0 reduce-scatter.5.cloned.1.call-update
  148.8 0.9 dynamic-slice_bitcast_fusion
  149.7 0.9 constant_dynamic-slice_fusion
  150.6 0.1 copy.10
  150.8 0.7 maximum_bitcast_fusion
  151.5 10.6 %reduce-scatter.5.cloned.1.call-done = bf16[4,384,64]{1,2,0:T(8,128)(2,1)} async-done(((bf16[4,384,128]{1,2,0:T(8,128)(2,1)}), bf16[4,384,64]{1,2,0:T(8,128)(2,1)}) %reduce-scatter.5.cloned.1.call-update) | async-done | bytes 196624 | tf_op jit(solution)/shard_map/reduce_scatter | solution.py:54
  162.1 0.0 copy-done
  162.1 0.0 copy-done.3
  162.1 2.2 %convolution_bitcast_fusion.2 = f32[4,384,64]{1,2,0:T(8,128)} fusion(bf16[4,384,384]{2,1,0:T(8,128)(2,1)S(1)} %copy-done, bf16[4,384,64]{1,2,0:T(8,128)(2,1)} %reduce-scatter.5.cloned.1.call-done, bf16[4,384,64]{1,2,0:T(8,128)(2,1)S(1)} %copy-done.3), kind=kOutput, calls=%fused_computation.5 | convolution fusion | flops 75890688 | bytes 1966080 | tf_op jit(solution)/shard_map/awv,avk->awk/dot_general | solution.py:58
Async XLA Ops:
  7.2 154.9 %copy-start = (bf16[4,384,384]{2,1,0:T(8,128)(2,1)S(1)}, bf16[4,384,384]{2,1,0:T(8,128)(2,1)}, u32[]{:S(2)}) copy-start(bf16[4,384,384]{2,1,0:T(8,128)(2,1)} %param.11) | copy-start | bytes 3538948
  7.2 55.4 %all-reduce.3.cloned.1.call-start = ((), (), s32[]{:S(2)}) async-start(), calls=%async_computation.2 | async-start | bytes 786432 | tf_op jit(solution)/shard_map/psum | solution.py:36
  17.8 0.8 copy-start.2
  22.0 3.4 %copy-start.1 = (f32[1536,512]{0,1:T(8,128)S(1)}, f32[1536,512]{0,1:T(8,128)}, u32[]{:S(2)}) copy-start(f32[1536,512]{0,1:T(8,128)} %convolution_bitcast_fusion.1) | copy-start | bytes 9437188
  29.1 7.4 %slice-start = ((bf16[1,2,1,384,512]{4,3,2,1,0:T(8,128)(2,1)}), bf16[1,1,1,384,512]{4,3,2,1,0:T(8,128)(2,1)S(1)}, s32[]{:S(2)}) async-start(bf16[1,2,1,384,512]{4,3,2,1,0:T(8,128)(2,1)} %param.6), calls=%async_computation.6 | async-start | bytes 786432 | tf_op jit(solution)/shard_map/slice | solution.py:30
  36.4 61.9 %all-reduce.5.cloned.1.call-start = ((), (), s32[]{:S(2)}) async-start(), calls=%async_computation.3 | async-start | bytes 786432 | tf_op jit(solution)/shard_map/psum | solution.py:9
  64.9 83.9 %reduce-scatter.3.cloned.1.call-start = ((), (), s32[]{:S(2)}) async-start(), calls=%async_computation.4 | async-start | bytes 1966080 | tf_op jit(solution)/shard_map/reduce_scatter | solution.py:51
  108.9 53.1 %copy-start.3 = (bf16[4,384,64]{1,2,0:T(8,128)(2,1)S(1)}, bf16[4,384,64]{1,2,0:T(8,128)(2,1)}, u32[]{:S(2)}) copy-start(bf16[4,384,64]{1,2,0:T(8,128)(2,1)} %param.10) | copy-start | bytes 589828
  112.2 49.8 %reduce-scatter.5.cloned.1.call-start = ((), (), s32[]{:S(2)}) async-start(), calls=%async_computation.5 | async-start | bytes 589824 | tf_op jit(solution)/shard_map/reduce_scatter | solution.py:54
Sparse Core Ops, SparseCore 0:
  36.5 26.0 all-reduce.2
  65.5 32.7 all-reduce.4
  112.3 36.4 reduce-scatter.2
  150.9 11.1 reduce-scatter.4
where the time goes:
time: 174 us; the launch traced here: 171 us
  waiting for transfers between devices  99 us (57%)
  between operations  28.8 us (17%)
  other arithmetic  16.2 us (9%)
  local copies, waits for them, and re-layouts  16 us (9%)
  matrix products  10.6 us (6%)
    reduce_scatter x1, waiting for transfers between devices, on_device(): lax.psum_scatter(ancestor_part.astype(jnp.bfloat16), 'layer', scatter_dim...  36.5 us
    psum x1, waiting for transfers between devices, broadcast(): return lax.psum(kept, axis)  26 us
    psum x1, waiting for transfers between devices, on_device(): lax.psum(collected[current].astype(jnp.bfloat16), 'col').astype(jnp.float32)  25.9 us
    dynamic_update_slice x7, other arithmetic, on_device(): lax.dynamic_update_index_in_dim(collected, before + product[member], targ...  15.5 us
    reduce_scatter x1, waiting for transfers between devices, on_device(): lax.psum_scatter(merged.astype(jnp.bfloat16), 'col', scatter_dimension=2,...  10.6 us
    dot_general x2, matrix products, on_device(): jnp.dot(stacked, answer, preferred_element_type=jnp.float32)  4.69 us
    dot_general x2, matrix products, solve_block(): jnp.dot(inverse, residual, preferred_element_type=jnp.float32)  3.69 us
  transfers between devices with their start and end apart: 4, of which 4 were waited for; matrix products, arithmetic and copies ran while one was open for 2% of the time, Pallas kernels for 0%

commit v1 on v0

v1 whole, which is shorter than its diff:
```python
import functools

import jax
import jax.numpy as jnp
from jax import lax
from jax.experimental import pallas as pl
from jax.experimental.pallas import tpu as pltpu
from jax.sharding import PartitionSpec as P

MESH = pl.DeviceIdType.MESH
F32 = jnp.float32
BF16 = jnp.bfloat16


def dot_t(left, right):
    return lax.dot_general(left, right, (((1,), (1,)), ((), ())), preferred_element_type=F32)


def kernel(
    sizes,
    targets,
    rhs_hbm,
    inv_hbm,
    blocks_hbm,
    rhs_anc_hbm,
    inv_anc_hbm,
    low_out,
    anc_out,
    rhs,
    inv,
    blocks0,
    blocks1,
    rhs_anc,
    inv_anc,
    low,
    x0,
    x1,
    part,
    part_in,
    right,
    base,
    packed,
    y_in,
    z_out,
    z_in,
    load_sem,
    out_sem,
    p_send,
    p_recv,
    x_send,
    x_recv,
    y_send,
    y_recv,
    z_send,
    z_recv,
):
    layers, rows, cols = sizes
    layer, row, col = (lax.axis_index(a) for a in ("layer", "row", "col"))
    slots = blocks0.shape[0]
    anc_row, narrow, width = rhs_anc.shape
    share = x1.shape[1]

    def ordered(k):
        return (row // 2 * 2 + k // 2 * 2) % rows + (row + k) % 2

    barrier = pltpu.get_barrier_semaphore()
    for dr in range(rows):
        for dc in range(cols):
            if dr or dc:
                pl.semaphore_signal(
                    barrier,
                    inc=1,
                    device_id={"row": (row + dr) % rows, "col": (col + dc) % cols},
                    device_id_type=MESH,
                )
    for dl in range(1, layers):
        pl.semaphore_signal(
            barrier, inc=1, device_id={"layer": (layer + dl) % layers}, device_id_type=MESH
        )

    loads = [
        pltpu.make_async_copy(inv_hbm.at[0], inv.at[0], load_sem.at[0]),
        pltpu.make_async_copy(rhs_hbm.at[0], rhs.at[0], load_sem.at[1]),
        pltpu.make_async_copy(blocks_hbm.at[0], blocks0, load_sem.at[2]),
        pltpu.make_async_copy(inv_hbm.at[1], inv.at[1], load_sem.at[3]),
        pltpu.make_async_copy(rhs_hbm.at[1], rhs.at[1], load_sem.at[4]),
        pltpu.make_async_copy(blocks_hbm.at[1], blocks1, load_sem.at[5]),
        pltpu.make_async_copy(inv_anc_hbm, inv_anc, load_sem.at[6]),
        pltpu.make_async_copy(rhs_anc_hbm, rhs_anc, load_sem.at[7]),
    ]
    for load in loads:
        load.start()

    def listed(level, target):
        index, found = jnp.int32(0), jnp.int32(0)
        for s in range(slots):
            hit = (targets[level, s] == target).astype(jnp.int32)
            index = index + hit * s
            found = found + hit
        return (blocks0, blocks1)[level][index], found.astype(F32)

    def span(j):
        return pl.ds(pl.multiple_of(j * share, share), share)

    loads[0].wait()
    loads[1].wait()
    first = jnp.dot(inv[0], rhs[0], preferred_element_type=F32)
    x0[...] = first.T.astype(BF16)

    loads[2].wait()
    goal = (row + rows - 1) % rows
    active = goal < cols
    owner = (1 + col) % rows

    def p_copy(k):
        j = ordered(k)
        return pltpu.make_async_remote_copy(
            src_ref=part.at[j],
            dst_ref=part_in.at[col],
            send_sem=p_send.at[k],
            recv_sem=p_recv.at[col],
            device_id={"row": j, "col": goal},
            device_id_type=MESH,
        )

    pl.semaphore_wait(barrier, rows * cols - 1 + layers - 1)

    @pl.when(active)
    def _():
        block, found = listed(0, 1)
        for k in range(rows):
            j = ordered(k)
            value = dot_t(x0[span(j), :], block) * found
            part[j] = value.astype(BF16)
            if k == 0:

                @pl.when(goal != col)
                def _():
                    p_copy(0).start()

                @pl.when(goal == col)
                def _():
                    part_in[col] = part[row]

            else:
                p_copy(k).start()

    for j in range(rows):

        @pl.when(row == j)
        def _():
            low[0] = x0[j * share : (j + 1) * share, :].astype(F32).T.astype(BF16)

    low0 = pltpu.make_async_copy(low.at[0], low_out.at[0], out_sem.at[0])
    low0.start()

    for a in range(anc_row):
        block, found = listed(0, a + 2)
        base[:, a * width : (a + 1) * width] = dot_t(x0[...], block) * found

    loads[3].wait()
    loads[4].wait()
    for j in range(rows):

        @pl.when(row == j)
        def _():
            right[...] = rhs[1, :, j * share : (j + 1) * share].astype(F32).T

    for cc in range(cols):

        @pl.when(jnp.logical_or(col != cc, row != owner))
        def _():
            pltpu.make_async_remote_copy(
                src_ref=part.at[0],
                dst_ref=part_in.at[cc],
                send_sem=p_send.at[0],
                recv_sem=p_recv.at[cc],
                device_id={"row": row, "col": col},
                device_id_type=MESH,
            ).wait_recv()

    total = part_in[0].astype(F32)
    for cc in range(1, cols):
        total = total + part_in[cc].astype(F32)
    residual = (right[...] - total).astype(BF16)
    x1[row] = dot_t(residual, inv[1]).astype(BF16)

    def x_copy(k, slot):
        return pltpu.make_async_remote_copy(
            src_ref=x1.at[slot],
            dst_ref=x1.at[slot],
            send_sem=x_send.at[k],
            recv_sem=x_recv.at[slot],
            device_id={"row": ordered(k)},
            device_id_type=MESH,
        )

    for k in range(1, rows):
        x_copy(k, row).start()

    def y_copy(d, j):
        cc = (col + d) % cols
        return pltpu.make_async_remote_copy(
            src_ref=packed.at[cc, j],
            dst_ref=y_in.at[d - 1, j],
            send_sem=y_send.at[d - 1, j],
            recv_sem=y_recv.at[d - 1, j],
            device_id={"col": cc},
            device_id_type=MESH,
        )

    loads[5].wait()
    for k in range(rows):
        j = ordered(k)
        if k:
            x_copy(k, j).wait_recv()
        for a in range(anc_row):
            block, found = listed(1, a + 2)
            at = slice(a * width, (a + 1) * width)
            value = base[span(j), at] + dot_t(x1[j], block) * found
            value = value.astype(BF16)
            for cc in range(cols):
                packed[cc, j, :, at] = value[cc * narrow : (cc + 1) * narrow]
        for d in range(1, cols):
            y_copy(d, j).start()
        if k == 0:
            low[1] = x1[row].astype(F32).T.astype(BF16)
            low1 = pltpu.make_async_copy(low.at[1], low_out.at[1], out_sem.at[1])
            low1.start()

    def z_copy(j):
        return pltpu.make_async_remote_copy(
            src_ref=z_out.at[j],
            dst_ref=z_in.at[layer],
            send_sem=z_send.at[j],
            recv_sem=z_recv.at[layer],
            device_id={"layer": j},
            device_id_type=MESH,
        )

    for k in range(rows):
        j = ordered(k)
        merged = packed[col, j].astype(F32)
        for d in range(1, cols):
            y_copy(d, j).wait_recv()
            merged = merged + y_in[d - 1, j].astype(F32)

        @pl.when(j != layer)
        def _():
            z_out[j] = merged.astype(BF16)
            z_copy(j).start()

        @pl.when(j == layer)
        def _():
            z_in[layer] = merged.astype(BF16)

    loads[6].wait()
    loads[7].wait()
    for s in range(layers):

        @pl.when(layer != s)
        def _():
            pltpu.make_async_remote_copy(
                src_ref=z_out.at[s],
                dst_ref=z_in.at[s],
                send_sem=z_send.at[s],
                recv_sem=z_recv.at[s],
                device_id={"layer": layer},
                device_id_type=MESH,
            ).wait_recv()

    for a in range(anc_row):
        residual = rhs_anc[a].astype(F32)
        for s in range(layers):
            residual = residual - z_in[s, :, a * width : (a + 1) * width].astype(F32)
        anc_out[a] = dot_t(residual.astype(BF16), inv_anc[a])

    @pl.when(active)
    def _():
        for k in range(rows):
            if k == 0:

                @pl.when(goal != col)
                def _():
                    p_copy(0).wait_send()

            else:
                p_copy(k).wait_send()

    for k in range(1, rows):
        x_copy(k, row).wait_send()
    for k in range(rows):
        j = ordered(k)
        for d in range(1, cols):
            y_copy(d, j).wait_send()

        @pl.when(j != layer)
        def _():
            z_copy(j).wait_send()

    low0.wait()
    low1.wait()


def on_device(sizes, rhs_low, inv_low, blocks, targets, rhs_anc, inv_anc):
    layers, rows, cols = sizes
    levels, slots = blocks.shape[3], blocks.shape[4]
    width, cases = rhs_low.shape[3], rhs_low.shape[4]
    anc_row, narrow = rhs_anc.shape[0], rhs_anc.shape[2]
    share = cases // rows
    assert levels == 2 and layers == rows and cols <= rows and cols * narrow == share
    any_space = pl.BlockSpec(memory_space=pl.ANY)
    dma = pltpu.SemaphoreType.DMA
    low, anc = pl.pallas_call(
        functools.partial(kernel, sizes),
        out_shape=(
            jax.ShapeDtypeStruct((levels, width, share), BF16),
            jax.ShapeDtypeStruct((anc_row, narrow, width), F32),
        ),
        in_specs=[pl.BlockSpec(memory_space=pltpu.SMEM)] + [any_space] * 5,
        out_specs=(any_space, pl.BlockSpec(memory_space=pltpu.VMEM)),
        scratch_shapes=[
            pltpu.VMEM((levels, width, cases), BF16),
            pltpu.VMEM((levels, width, width), BF16),
            pltpu.VMEM((slots, width, width), BF16),
            pltpu.VMEM((slots, width, width), BF16),
            pltpu.VMEM((anc_row, narrow, width), BF16),
            pltpu.VMEM((anc_row, width, width), BF16),
            pltpu.VMEM((levels, width, share), BF16),
            pltpu.VMEM((cases, width), BF16),
            pltpu.VMEM((rows, share, width), BF16),
            pltpu.VMEM((rows, share, width), BF16),
            pltpu.VMEM((cols, share, width), BF16),
            pltpu.VMEM((share, width), F32),
            pltpu.VMEM((cases, anc_row * width), F32),
            pltpu.VMEM((cols, rows, narrow, anc_row * width), BF16),
            pltpu.VMEM((cols - 1, rows, narrow, anc_row * width), BF16),
            pltpu.VMEM((layers, narrow, anc_row * width), BF16),
            pltpu.VMEM((layers, narrow, anc_row * width), BF16),
            dma((8,)),
            dma((2,)),
            dma((rows,)),
            dma((cols,)),
            dma((rows,)),
            dma((rows,)),
            dma((cols - 1, rows)),
            dma((cols - 1, rows)),
            dma((layers,)),
            dma((layers,)),
        ],
        compiler_params=pltpu.CompilerParams(
            collective_id=0, has_side_effects=True, vmem_limit_bytes=56 * 1024 * 1024
        ),
    )(
        targets.reshape(levels, slots),
        rhs_low.reshape(levels, width, cases),
        inv_low.reshape(levels, width, width),
        blocks.reshape(levels, slots, width, width),
        rhs_anc.transpose(0, 2, 1),
        inv_anc,
    )
    return low[None, :, None], anc.transpose(0, 2, 1)


def solution(mesh):
    sizes = tuple(mesh.shape[a] for a in ("layer", "row", "col"))
    in_specs = (
        P("layer", None, "col", None, None),
        P("layer", None, "col", None, None),
        P("layer", "row", "col", None, None, None, None),
        P("layer", "row", "col", None, None),
        P("row", None, ("layer", "col")),
        P("row", None, None),
    )
    out_specs = (P("layer", None, "col", None, "row"), P("row", None, ("layer", "col")))
    return jax.shard_map(
        functools.partial(on_device, sizes),
        mesh=mesh,
        in_specs=in_specs,
        out_specs=out_specs,
        check_vma=False,
    )
```

time: 174 us -> 49 us (0.28)
  the two profiles are of different devices: /device:TPU:6 before, /device:TPU:24 now
where the time goes in v1:
time: 49 us; the launch traced here: 48.8 us
  Pallas kernels  44.8 us (91%)
  local copies, waits for them, and re-layouts  3.39 us (7%)
  between operations  0.64 us (1%)
    pallas_call x1, Pallas kernels, on_device(): pl.pallas_call(functools.partial(kernel, sizes), out_shape=(jax.ShapeDtyp...  44.8 us
    unnamed x2, local copies, waits for them, and re-layouts  3.39 us

profile of v1, /device:TPU:24, one launch (start us, length us, event | category | flops | bytes accessed | tf_op | source)
XLA Modules:
  0.0 48.8 jit_solution(5370110084510363383)
XLA Ops:
  0.6 44.8 %shard_map.77 = (bf16[2,384,128]{2,1,0:T(8,128)(2,1)}, f32[4,64,384]{2,1,0:T(8,128)}) custom-call(s32[2,4]{1,0:T(2,128)} %bitcast.15, bf16[2,384,512]{2,1,0:T(8,128)(2,1)} %bitcast.10, bf16[2,384,384]{2,1,0:T(8,128)(2,1)} %bitcast.11, bf16[2,4,384,384]{3,2,1,0:T(8,128)(2,1)} %bitcast.9, bf16[4,64,384]{2,1,0:T(8,128)(2,1)} %bitcast.13, ...), custom_call_target="tpu_custom_call" | custom-call | tf_op jit(solution)/shard_map/pallas_call | solution.py:314
  45.4 1.6 %copy.11 = bf16[1,2,1,384,128]{4,3,2,1,0:T(8,128)(2,1)} copy(bf16[1,2,1,384,128]{4,3,2,1,0:T(8,128)(2,1)} %bitcast.14) | data formatting | bytes 393216
  47.0 1.8 %copy.12 = f32[4,384,64]{1,2,0:T(8,128)} copy(f32[4,384,64]{1,2,0:T(8,128)} %bitcast.12) | data formatting | bytes 786432

commit v2 on v1

--- a/solution.py
+++ b/solution.py
@@ -63,6 +63,31 @@
     def ordered(k):
         return (row // 2 * 2 + k // 2 * 2) % rows + (row + k) % 2
 
+    def flag(condition):
+        return condition.astype(jnp.int32)
+
+    last = layers - 1
+    relayed = flag(layer == 1) * last - flag(layer != 1)
+    relayed = relayed + flag(layer == last - 1) * (0 - relayed)
+    opening = row + flag(row == layer) * (ordered(1) - row)
+    keys = []
+    for j in range(rows):
+        place = 0
+        for k in range(rows):
+            place = place + k * flag(ordered(k) == j)
+        key = place - 16 * jnp.abs(layer - j)
+        key = key + 500 * flag(relayed == j) + 5000 * flag(layer == j) - 2000 * flag(opening == j)
+        keys.append(key)
+    order = [0] * rows
+    for j in range(rows):
+        rank = 0
+        for other in range(rows):
+            if other != j:
+                rank = rank + flag(keys[other] < keys[j])
+        order = [order[k] + j * flag(rank == k) for k in range(rows)]
+    swap = flag(relayed == opening) * (order[1] - order[0])
+    merge_order = [order[0] + swap, order[1] - swap] + order[2:]
+
     barrier = pltpu.get_barrier_semaphore()
     for dr in range(rows):
         for dc in range(cols):
@@ -211,9 +236,12 @@
 
     loads[5].wait()
     for k in range(rows):
-        j = ordered(k)
-        if k:
-            x_copy(k, j).wait_recv()
+        j = order[k]
+
+        @pl.when(j != row)
+        def _():
+            x_copy(1, j).wait_recv()
+
         for a in range(anc_row):
             block, found = listed(1, a + 2)
             at = slice(a * width, (a + 1) * width)
@@ -228,27 +256,53 @@
             low1 = pltpu.make_async_copy(low.at[1], low_out.at[1], out_sem.at[1])
             low1.start()
 
-    def z_copy(j):
+    def z_copy(j, slot, target):
         return pltpu.make_async_remote_copy(
             src_ref=z_out.at[j],
-            dst_ref=z_in.at[layer],
+            dst_ref=z_in.at[slot],
             send_sem=z_send.at[j],
-            recv_sem=z_recv.at[layer],
-            device_id={"layer": j},
+            recv_sem=z_recv.at[slot],
+            device_id={"layer": target},
             device_id_type=MESH,
         )
 
     for k in range(rows):
-        j = ordered(k)
+        j = merge_order[k]
+        for d in range(1, cols):
+            y_copy(d, j).wait_recv()
         merged = packed[col, j].astype(F32)
         for d in range(1, cols):
-            y_copy(d, j).wait_recv()
             merged = merged + y_in[d - 1, j].astype(F32)
 
-        @pl.when(j != layer)
+        @pl.when(jnp.logical_and(j == last, layer == 1))
+        def _():
+            z_copy(j, layers, layer).wait_recv()
+            z_out[j] = (merged + z_in[layers].astype(F32)).astype(BF16)
+            z_copy(j, layer, j).start()
+
+        @pl.when(jnp.logical_and(j == 0, layer == last - 1))
+        def _():
+            z_copy(j, layers + 1, layer).wait_recv()
+            z_out[j] = (merged + z_in[layers + 1].astype(F32)).astype(BF16)
+            z_copy(j, layer, j).start()
+
+        @pl.when(jnp.logical_and(j == last, layer == 0))
         def _():
             z_out[j] = merged.astype(BF16)
-            z_copy(j).start()
+            z_copy(j, layers, 1).start()
+
+        @pl.when(jnp.logical_and(j == 0, layer == last))
+        def _():
+            z_out[j] = merged.astype(BF16)
+            z_copy(j, layers + 1, last - 1).start()
+
+        direct = jnp.logical_and(j != layer, j != relayed)
+        direct = jnp.logical_and(direct, jnp.abs(layer - j) != last)
+
+        @pl.when(direct)
+        def _():
+            z_out[j] = merged.astype(BF16)
+            z_copy(j, layer, j).start()
 
         @pl.when(j == layer)
         def _():
@@ -258,16 +312,13 @@
     loads[7].wait()
     for s in range(layers):
 
-        @pl.when(layer != s)
-        def _():
-            pltpu.make_async_remote_copy(
-                src_ref=z_out.at[s],
-                dst_ref=z_in.at[s],
-                send_sem=z_send.at[s],
-                recv_sem=z_recv.at[s],
-                device_id={"layer": layer},
-                device_id_type=MESH,
-            ).wait_recv()
+        @pl.when(jnp.abs(layer - s) == last)
+        def _():
+            z_in[s] = jnp.zeros_like(z_in[s])
+
+        @pl.when(jnp.logical_and(layer != s, jnp.abs(layer - s) != last))
+        def _():
+            z_copy(s, s, layer).wait_recv()
 
     for a in range(anc_row):
         residual = rhs_anc[a].astype(F32)
@@ -296,7 +347,7 @@
 
         @pl.when(j != layer)
         def _():
-            z_copy(j).wait_send()
+            z_copy(j, layer, j).wait_send()
 
     low0.wait()
     low1.wait()
@@ -308,7 +359,7 @@
     width, cases = rhs_low.shape[3], rhs_low.shape[4]
     anc_row, narrow = rhs_anc.shape[0], rhs_anc.shape[2]
     share = cases // rows
-    assert levels == 2 and layers == rows and cols <= rows and cols * narrow == share
+    assert levels == 2 and layers == rows and layers > 3 and cols <= rows and cols * narrow == share
     any_space = pl.BlockSpec(memory_space=pl.ANY)
     dma = pltpu.SemaphoreType.DMA
     low, anc = pl.pallas_call(
@@ -336,7 +387,7 @@
             pltpu.VMEM((cols, rows, narrow, anc_row * width), BF16),
             pltpu.VMEM((cols - 1, rows, narrow, anc_row * width), BF16),
             pltpu.VMEM((layers, narrow, anc_row * width), BF16),
-            pltpu.VMEM((layers, narrow, anc_row * width), BF16),
+            pltpu.VMEM((layers + 2, narrow, anc_row * width), BF16),
             dma((8,)),
             dma((2,)),
             dma((rows,)),
@@ -346,7 +397,7 @@
             dma((cols - 1, rows)),
             dma((cols - 1, rows)),
             dma((layers,)),
-            dma((layers,)),
+            dma((layers + 2,)),
         ],
         compiler_params=pltpu.CompilerParams(
             collective_id=0, has_side_effects=True, vmem_limit_bytes=56 * 1024 * 1024

time: 49 us -> 43 us (0.88)
  the two profiles are of different devices: /device:TPU:24 before, /device:TPU:6 now
where the time goes in v2:
time: 43 us; the launch traced here: 42.6 us
  Pallas kernels  38.5 us (90%)
  local copies, waits for them, and re-layouts  3.39 us (8%)
  between operations  0.64 us (1%)
    pallas_call x1, Pallas kernels, on_device(): pl.pallas_call(functools.partial(kernel, sizes), out_shape=(jax.ShapeDtyp...  38.5 us
    unnamed x2, local copies, waits for them, and re-layouts  3.39 us

profile of v2, /device:TPU:6, one launch (start us, length us, event | category | flops | bytes accessed | tf_op | source)
XLA Modules:
  0.0 42.6 jit_solution(273441391405538467)
XLA Ops:
  0.6 38.5 %shard_map.77 = (bf16[2,384,128]{2,1,0:T(8,128)(2,1)}, f32[4,64,384]{2,1,0:T(8,128)}) custom-call(s32[2,4]{1,0:T(2,128)} %bitcast.15, bf16[2,384,512]{2,1,0:T(8,128)(2,1)} %bitcast.10, bf16[2,384,384]{2,1,0:T(8,128)(2,1)} %bitcast.11, bf16[2,4,384,384]{3,2,1,0:T(8,128)(2,1)} %bitcast.9, bf16[4,64,384]{2,1,0:T(8,128)(2,1)} %bitcast.13, ...), custom_call_target="tpu_custom_call" | custom-call | tf_op jit(solution)/shard_map/pallas_call | solution.py:365
  39.2 1.6 %copy.11 = bf16[1,2,1,384,128]{4,3,2,1,0:T(8,128)(2,1)} copy(bf16[1,2,1,384,128]{4,3,2,1,0:T(8,128)(2,1)} %bitcast.14) | data formatting | bytes 393216
  40.8 1.8 %copy.12 = f32[4,384,64]{1,2,0:T(8,128)} copy(f32[4,384,64]{1,2,0:T(8,128)} %bitcast.12) | data formatting | bytes 786432

commit v3 on v2

--- a/solution.py
+++ b/solution.py
@@ -32,7 +32,6 @@
     blocks1,
     rhs_anc,
     inv_anc,
-    low,
     x0,
     x1,
     part,
@@ -44,7 +43,6 @@
     z_out,
     z_in,
     load_sem,
-    out_sem,
     p_send,
     p_recv,
     x_send,
@@ -174,10 +172,7 @@
 
         @pl.when(row == j)
         def _():
-            low[0] = x0[j * share : (j + 1) * share, :].astype(F32).T.astype(BF16)
-
-    low0 = pltpu.make_async_copy(low.at[0], low_out.at[0], out_sem.at[0])
-    low0.start()
+            low_out[0] = x0[j * share : (j + 1) * share, :].astype(F32).T.astype(BF16)
 
     for a in range(anc_row):
         block, found = listed(0, a + 2)
@@ -252,9 +247,7 @@
         for d in range(1, cols):
             y_copy(d, j).start()
         if k == 0:
-            low[1] = x1[row].astype(F32).T.astype(BF16)
-            low1 = pltpu.make_async_copy(low.at[1], low_out.at[1], out_sem.at[1])
-            low1.start()
+            low_out[1] = x1[row].astype(F32).T.astype(BF16)
 
     def z_copy(j, slot, target):
         return pltpu.make_async_remote_copy(
@@ -326,6 +319,7 @@
             residual = residual - z_in[s, :, a * width : (a + 1) * width].astype(F32)
         anc_out[a] = dot_t(residual.astype(BF16), inv_anc[a])
 
+
     @pl.when(active)
     def _():
         for k in range(rows):
@@ -349,8 +343,14 @@
         def _():
             z_copy(j, layer, j).wait_send()
 
-    low0.wait()
-    low1.wait()
+
+def hand_over(low, anc, low_out, anc_out, sem):
+    first = pltpu.make_async_copy(anc, anc_out, sem.at[0])
+    second = pltpu.make_async_copy(low, low_out, sem.at[1])
+    first.start()
+    second.start()
+    first.wait()
+    second.wait()
 
 
 def on_device(sizes, rhs_low, inv_low, blocks, targets, rhs_anc, inv_anc):
@@ -360,16 +360,16 @@
     anc_row, narrow = rhs_anc.shape[0], rhs_anc.shape[2]
     share = cases // rows
     assert levels == 2 and layers == rows and layers > 3 and cols <= rows and cols * narrow == share
-    any_space = pl.BlockSpec(memory_space=pl.ANY)
+    any_space = pl.BlockSpec(memory_space=pltpu.HBM)
     dma = pltpu.SemaphoreType.DMA
     low, anc = pl.pallas_call(
         functools.partial(kernel, sizes),
         out_shape=(
-            jax.ShapeDtypeStruct((levels, width, share), BF16),
-            jax.ShapeDtypeStruct((anc_row, narrow, width), F32),
+            pltpu.VMEM((levels, width, share), BF16),
+            pltpu.VMEM((anc_row, narrow, width), F32),
         ),
         in_specs=[pl.BlockSpec(memory_space=pltpu.SMEM)] + [any_space] * 5,
-        out_specs=(any_space, pl.BlockSpec(memory_space=pltpu.VMEM)),
+        out_specs=(pl.BlockSpec(memory_space=pltpu.VMEM), pl.BlockSpec(memory_space=pltpu.VMEM)),
         scratch_shapes=[
             pltpu.VMEM((levels, width, cases), BF16),
             pltpu.VMEM((levels, width, width), BF16),
@@ -377,7 +377,6 @@
             pltpu.VMEM((slots, width, width), BF16),
             pltpu.VMEM((anc_row, narrow, width), BF16),
             pltpu.VMEM((anc_row, width, width), BF16),
-            pltpu.VMEM((levels, width, share), BF16),
             pltpu.VMEM((cases, width), BF16),
             pltpu.VMEM((rows, share, width), BF16),
             pltpu.VMEM((rows, share, width), BF16),
@@ -389,7 +388,6 @@
             pltpu.VMEM((layers, narrow, anc_row * width), BF16),
             pltpu.VMEM((layers + 2, narrow, anc_row * width), BF16),
             dma((8,)),
-            dma((2,)),
             dma((rows,)),
             dma((cols,)),
             dma((rows,)),
@@ -410,6 +408,17 @@
         rhs_anc.transpose(0, 2, 1),
         inv_anc,
     )
+    low, anc = pl.pallas_call(
+        hand_over,
+        out_shape=(
+            jax.ShapeDtypeStruct(low.shape, low.dtype),
+            jax.ShapeDtypeStruct(anc.shape, anc.dtype),
+        ),
+        in_specs=[pl.BlockSpec(memory_space=pltpu.VMEM)] * 2,
+        out_specs=(any_space, any_space),
+        scratch_shapes=[dma((2,))],
+        compiler_params=pltpu.CompilerParams(vmem_limit_bytes=4 * 1024 * 1024),
+    )(low, anc)
     return low[None, :, None], anc.transpose(0, 2, 1)
 
 

time: 43 us -> 39.6 us (0.921)
  local copies, waits for them, and re-layouts: 3.39 us -> 0 us
    unnamed x2 -> x0, local copies, waits for them, and re-layouts: 3.39 us -> none
    pallas_call x1 -> x2, Pallas kernels: 38.5 us -> 38.6 us  [the longest x1 37.8 us: on_device(): pl.pallas_call(functools.partial(kernel, sizes), out_shape=(pltpu.VMEM((l...]
where the time goes in v3:
time: 39.6 us; the launch traced here: 39.3 us
  Pallas kernels  38.6 us (97%)
  between operations  0.64 us (2%)
    pallas_call x1, Pallas kernels, on_device(): pl.pallas_call(functools.partial(kernel, sizes), out_shape=(pltpu.VMEM((l...  37.8 us
    pallas_call x1, Pallas kernels, on_device(): pl.pallas_call(hand_over, out_shape=(jax.ShapeDtypeStruct(low.shape, low....  0.83 us

profile of v3, /device:TPU:6, one launch (start us, length us, event | category | flops | bytes accessed | tf_op | source)
XLA Modules:
  0.0 39.3 jit_solution(15612905685145347923)
XLA Ops:
  0.6 37.8 %shard_map.77 = (bf16[2,384,128]{2,1,0:T(8,128)(2,1)S(1)}, f32[4,64,384]{2,1,0:T(8,128)S(1)}) custom-call(s32[2,4]{1,0:T(2,128)} %bitcast.13, bf16[2,384,512]{2,1,0:T(8,128)(2,1)} %bitcast.10, bf16[2,384,384]{2,1,0:T(8,128)(2,1)} %bitcast.11, bf16[2,4,384,384]{3,2,1,0:T(8,128)(2,1)} %bitcast.9, bf16[4,64,384]{2,1,0:T(8,128)(2,1)} %bitcast.12, ...), custom_call_target="tpu_custom_call" | custom-call | tf_op jit(solution)/shard_map/pallas_call | solution.py:365
  38.4 0.8 %shard_map.78 = (bf16[2,384,128]{2,1,0:T(8,128)(2,1)}, f32[4,64,384]{2,1,0:T(8,128)}) custom-call(bf16[2,384,128]{2,1,0:T(8,128)(2,1)S(1)} %get-tuple-element.6.low, f32[4,64,384]{2,1,0:T(8,128)S(1)} %get-tuple-element.7.anc), custom_call_target="tpu_custom_call" | custom-call | tf_op jit(solution)/shard_map/pallas_call | solution.py:411

commit v4 on v3

--- a/solution.py
+++ b/solution.py
@@ -18,7 +18,7 @@
 
 def kernel(
     sizes,
-    targets,
+    targets_hbm,
     rhs_hbm,
     inv_hbm,
     blocks_hbm,
@@ -42,6 +42,7 @@
     y_in,
     z_out,
     z_in,
+    targets,
     load_sem,
     p_send,
     p_recv,
@@ -57,6 +58,8 @@
     slots = blocks0.shape[0]
     anc_row, narrow, width = rhs_anc.shape
     share = x1.shape[1]
+    halves = packed.shape[2]
+    per_half = anc_row // halves
 
     def ordered(k):
         return (row // 2 * 2 + k // 2 * 2) % rows + (row + k) % 2
@@ -110,6 +113,7 @@
         pltpu.make_async_copy(blocks_hbm.at[1], blocks1, load_sem.at[5]),
         pltpu.make_async_copy(inv_anc_hbm, inv_anc, load_sem.at[6]),
         pltpu.make_async_copy(rhs_anc_hbm, rhs_anc, load_sem.at[7]),
+        pltpu.make_async_copy(targets_hbm, targets, load_sem.at[8]),
     ]
     for load in loads:
         load.start()
@@ -130,6 +134,7 @@
     first = jnp.dot(inv[0], rhs[0], preferred_element_type=F32)
     x0[...] = first.T.astype(BF16)
 
+    loads[8].wait()
     loads[2].wait()
     goal = (row + rows - 1) % rows
     active = goal < cols
@@ -218,13 +223,13 @@
     for k in range(1, rows):
         x_copy(k, row).start()
 
-    def y_copy(d, j):
+    def y_copy(d, j, h):
         cc = (col + d) % cols
         return pltpu.make_async_remote_copy(
-            src_ref=packed.at[cc, j],
-            dst_ref=y_in.at[d - 1, j],
-            send_sem=y_send.at[d - 1, j],
-            recv_sem=y_recv.at[d - 1, j],
+            src_ref=packed.at[cc, j, h],
+            dst_ref=y_in.at[d - 1, j, h],
+            send_sem=y_send.at[d - 1, j, h],
+            recv_sem=y_recv.at[d - 1, j, h],
             device_id={"col": cc},
             device_id_type=MESH,
         )
@@ -243,63 +248,70 @@
             value = base[span(j), at] + dot_t(x1[j], block) * found
             value = value.astype(BF16)
             for cc in range(cols):
-                packed[cc, j, :, at] = value[cc * narrow : (cc + 1) * narrow]
-        for d in range(1, cols):
-            y_copy(d, j).start()
+                within = a % per_half * width
+                packed[cc, j, a // per_half, :, within : within + width] = value[
+                    cc * narrow : (cc + 1) * narrow
+                ]
+            if a % per_half == per_half - 1:
+                for d in range(1, cols):
+                    y_copy(d, j, a // per_half).start()
         if k == 0:
             low_out[1] = x1[row].astype(F32).T.astype(BF16)
 
-    def z_copy(j, slot, target):
+    def z_copy(j, slot, target, h):
         return pltpu.make_async_remote_copy(
-            src_ref=z_out.at[j],
-            dst_ref=z_in.at[slot],
-            send_sem=z_send.at[j],
-            recv_sem=z_recv.at[slot],
+            src_ref=z_out.at[j, h],
+            dst_ref=z_in.at[slot, h],
+            send_sem=z_send.at[j, h],
+            recv_sem=z_recv.at[slot, h],
             device_id={"layer": target},
             device_id_type=MESH,
         )
 
-    for k in range(rows):
-        j = merge_order[k]
+    def merge(j, h):
         for d in range(1, cols):
-            y_copy(d, j).wait_recv()
-        merged = packed[col, j].astype(F32)
+            y_copy(d, j, h).wait_recv()
+        merged = packed[col, j, h].astype(F32)
         for d in range(1, cols):
-            merged = merged + y_in[d - 1, j].astype(F32)
+            merged = merged + y_in[d - 1, j, h].astype(F32)
 
         @pl.when(jnp.logical_and(j == last, layer == 1))
         def _():
-            z_copy(j, layers, layer).wait_recv()
-            z_out[j] = (merged + z_in[layers].astype(F32)).astype(BF16)
-            z_copy(j, layer, j).start()
+            z_copy(j, layers, layer, h).wait_recv()
+            z_out[j, h] = (merged + z_in[layers, h].astype(F32)).astype(BF16)
+            z_copy(j, layer, j, h).start()
 
         @pl.when(jnp.logical_and(j == 0, layer == last - 1))
         def _():
-            z_copy(j, layers + 1, layer).wait_recv()
-            z_out[j] = (merged + z_in[layers + 1].astype(F32)).astype(BF16)
-            z_copy(j, layer, j).start()
+            z_copy(j, layers + 1, layer, h).wait_recv()
+            z_out[j, h] = (merged + z_in[layers + 1, h].astype(F32)).astype(BF16)
+            z_copy(j, layer, j, h).start()
 
         @pl.when(jnp.logical_and(j == last, layer == 0))
         def _():
-            z_out[j] = merged.astype(BF16)
-            z_copy(j, layers, 1).start()
+            z_out[j, h] = merged.astype(BF16)
+            z_copy(j, layers, 1, h).start()
 
         @pl.when(jnp.logical_and(j == 0, layer == last))
         def _():
-            z_out[j] = merged.astype(BF16)
-            z_copy(j, layers + 1, last - 1).start()
+            z_out[j, h] = merged.astype(BF16)
+            z_copy(j, layers + 1, last - 1, h).start()
 
         direct = jnp.logical_and(j != layer, j != relayed)
         direct = jnp.logical_and(direct, jnp.abs(layer - j) != last)
 
         @pl.when(direct)
         def _():
-            z_out[j] = merged.astype(BF16)
-            z_copy(j, layer, j).start()
+            z_out[j, h] = merged.astype(BF16)
+            z_copy(j, layer, j, h).start()
 
         @pl.when(j == layer)
         def _():
-            z_in[layer] = merged.astype(BF16)
+            z_in[layer, h] = merged.astype(BF16)
+
+    for j in merge_order:
+        for h in range(halves):
+            merge(j, h)
 
     loads[6].wait()
     loads[7].wait()
@@ -311,12 +323,15 @@
 
         @pl.when(jnp.logical_and(layer != s, jnp.abs(layer - s) != last))
         def _():
-            z_copy(s, s, layer).wait_recv()
+            for h in range(halves):
+                z_copy(s, s, layer, h).wait_recv()
 
     for a in range(anc_row):
         residual = rhs_anc[a].astype(F32)
         for s in range(layers):
-            residual = residual - z_in[s, :, a * width : (a + 1) * width].astype(F32)
+            within = a % per_half * width
+            piece = z_in[s, a // per_half, :, within : within + width]
+            residual = residual - piece.astype(F32)
         anc_out[a] = dot_t(residual.astype(BF16), inv_anc[a])
 
 
@@ -337,11 +352,13 @@
     for k in range(rows):
         j = ordered(k)
         for d in range(1, cols):
-            y_copy(d, j).wait_send()
+            for h in range(halves):
+                y_copy(d, j, h).wait_send()
 
         @pl.when(j != layer)
         def _():
-            z_copy(j, layer, j).wait_send()
+            for h in range(halves):
+                z_copy(j, layer, j, h).wait_send()
 
 
 def hand_over(low, anc, low_out, anc_out, sem):
@@ -359,6 +376,7 @@
     width, cases = rhs_low.shape[3], rhs_low.shape[4]
     anc_row, narrow = rhs_anc.shape[0], rhs_anc.shape[2]
     share = cases // rows
+    halves = 2 if anc_row % 2 == 0 else 1
     assert levels == 2 and layers == rows and layers > 3 and cols <= rows and cols * narrow == share
     any_space = pl.BlockSpec(memory_space=pltpu.HBM)
     dma = pltpu.SemaphoreType.DMA
@@ -368,7 +386,7 @@
             pltpu.VMEM((levels, width, share), BF16),
             pltpu.VMEM((anc_row, narrow, width), F32),
         ),
-        in_specs=[pl.BlockSpec(memory_space=pltpu.SMEM)] + [any_space] * 5,
+        in_specs=[any_space] * 6,
         out_specs=(pl.BlockSpec(memory_space=pltpu.VMEM), pl.BlockSpec(memory_space=pltpu.VMEM)),
         scratch_shapes=[
             pltpu.VMEM((levels, width, cases), BF16),
@@ -383,19 +401,20 @@
             pltpu.VMEM((cols, share, width), BF16),
             pltpu.VMEM((share, width), F32),
             pltpu.VMEM((cases, anc_row * width), F32),
-            pltpu.VMEM((cols, rows, narrow, anc_row * width), BF16),
-            pltpu.VMEM((cols - 1, rows, narrow, anc_row * width), BF16),
-            pltpu.VMEM((layers, narrow, anc_row * width), BF16),
-            pltpu.VMEM((layers + 2, narrow, anc_row * width), BF16),
-            dma((8,)),
+            pltpu.VMEM((cols, rows, halves, narrow, anc_row * width // halves), BF16),
+            pltpu.VMEM((cols - 1, rows, halves, narrow, anc_row * width // halves), BF16),
+            pltpu.VMEM((layers, halves, narrow, anc_row * width // halves), BF16),
+            pltpu.VMEM((layers + 2, halves, narrow, anc_row * width // halves), BF16),
+            pltpu.SMEM((levels, slots), jnp.int32),
+            dma((9,)),
             dma((rows,)),
             dma((cols,)),
             dma((rows,)),
             dma((rows,)),
-            dma((cols - 1, rows)),
-            dma((cols - 1, rows)),
-            dma((layers,)),
-            dma((layers + 2,)),
+            dma((cols - 1, rows, halves)),
+            dma((cols - 1, rows, halves)),
+            dma((layers, halves)),
+            dma((layers + 2, halves)),
         ],
         compiler_params=pltpu.CompilerParams(
             collective_id=0, has_side_effects=True, vmem_limit_bytes=56 * 1024 * 1024

time: 39.6 us -> 38.5 us (0.972)
  Pallas kernels: 38.6 us -> 37.7 us
    pallas_call x1, Pallas kernels: 37.8 us -> 36.9 us  [on_device(): pl.pallas_call(functools.partial(kernel, sizes), out_shape=(pltpu.VMEM((l...]
where the time goes in v4:
time: 38.5 us; the launch traced here: 38.4 us
  Pallas kernels  37.7 us (98%)
  between operations  0.64 us (2%)
    pallas_call x1, Pallas kernels, on_device(): pl.pallas_call(functools.partial(kernel, sizes), out_shape=(pltpu.VMEM((l...  36.9 us
    pallas_call x1, Pallas kernels, on_device(): pl.pallas_call(hand_over, out_shape=(jax.ShapeDtypeStruct(low.shape, low....  0.83 us

profile of v4, /device:TPU:6, one launch (start us, length us, event | category | flops | bytes accessed | tf_op | source)
XLA Modules:
  0.0 38.4 jit_solution(12424388328412082383)
XLA Ops:
  0.6 36.9 %shard_map.77 = (bf16[2,384,128]{2,1,0:T(8,128)(2,1)S(1)}, f32[4,64,384]{2,1,0:T(8,128)S(1)}) custom-call(s32[2,4]{1,0:T(2,128)} %bitcast.13, bf16[2,384,512]{2,1,0:T(8,128)(2,1)} %bitcast.10, bf16[2,384,384]{2,1,0:T(8,128)(2,1)} %bitcast.11, bf16[2,4,384,384]{3,2,1,0:T(8,128)(2,1)} %bitcast.9, bf16[4,64,384]{2,1,0:T(8,128)(2,1)} %bitcast.12, ...), custom_call_target="tpu_custom_call" | custom-call | tf_op jit(solution)/shard_map/pallas_call | solution.py:383
  37.5 0.8 %shard_map.78 = (bf16[2,384,128]{2,1,0:T(8,128)(2,1)}, f32[4,64,384]{2,1,0:T(8,128)}) custom-call(bf16[2,384,128]{2,1,0:T(8,128)(2,1)S(1)} %get-tuple-element.6.low, f32[4,64,384]{2,1,0:T(8,128)S(1)} %get-tuple-element.7.anc), custom_call_target="tpu_custom_call" | custom-call | tf_op jit(solution)/shard_map/pallas_call | solution.py:430

commit v5 on v4

--- a/solution.py
+++ b/solution.py
@@ -376,7 +376,7 @@
     width, cases = rhs_low.shape[3], rhs_low.shape[4]
     anc_row, narrow = rhs_anc.shape[0], rhs_anc.shape[2]
     share = cases // rows
-    halves = 2 if anc_row % 2 == 0 else 1
+    halves = anc_row
     assert levels == 2 and layers == rows and layers > 3 and cols <= rows and cols * narrow == share
     any_space = pl.BlockSpec(memory_space=pltpu.HBM)
     dma = pltpu.SemaphoreType.DMA

time: 38.5 us -> 39.3 us (1.021)
  Pallas kernels: 37.7 us -> 38.2 us
    pallas_call x1, Pallas kernels: 36.9 us -> 37.4 us  [on_device(): pl.pallas_call(functools.partial(kernel, sizes), out_shape=(pltpu.VMEM((l...]
where the time goes in v5:
time: 39.3 us; the launch traced here: 38.9 us
  Pallas kernels  38.2 us (97%)
  between operations  0.64 us (2%)
    pallas_call x1, Pallas kernels, on_device(): pl.pallas_call(functools.partial(kernel, sizes), out_shape=(pltpu.VMEM((l...  37.4 us
    pallas_call x1, Pallas kernels, on_device(): pl.pallas_call(hand_over, out_shape=(jax.ShapeDtypeStruct(low.shape, low....  0.83 us

profile of v5, /device:TPU:6, one launch (start us, length us, event | category | flops | bytes accessed | tf_op | source)
XLA Modules:
  0.0 38.9 jit_solution(4626384274578981595)
XLA Ops:
  0.6 37.4 %shard_map.77 = (bf16[2,384,128]{2,1,0:T(8,128)(2,1)S(1)}, f32[4,64,384]{2,1,0:T(8,128)S(1)}) custom-call(s32[2,4]{1,0:T(2,128)} %bitcast.13, bf16[2,384,512]{2,1,0:T(8,128)(2,1)} %bitcast.10, bf16[2,384,384]{2,1,0:T(8,128)(2,1)} %bitcast.11, bf16[2,4,384,384]{3,2,1,0:T(8,128)(2,1)} %bitcast.9, bf16[4,64,384]{2,1,0:T(8,128)(2,1)} %bitcast.12, ...), custom_call_target="tpu_custom_call" | custom-call | tf_op jit(solution)/shard_map/pallas_call | solution.py:383
  38.0 0.8 %shard_map.78 = (bf16[2,384,128]{2,1,0:T(8,128)(2,1)}, f32[4,64,384]{2,1,0:T(8,128)}) custom-call(bf16[2,384,128]{2,1,0:T(8,128)(2,1)S(1)} %get-tuple-element.6.low, f32[4,64,384]{2,1,0:T(8,128)S(1)} %get-tuple-element.7.anc), custom_call_target="tpu_custom_call" | custom-call | tf_op jit(solution)/shard_map/pallas_call | solution.py:430
